TPU v7x, 256 devices: a whole 4x4x8 slice. The times are simulated.
256 devices in a mesh: seq: 64 (over z, x, core), tp: 4 (over y).
Axes of the slice: x: 4, y: 4, z: 8, core: 2. Of those that a mesh axis runs over, the one named last changes fastest.
Arguments:
- tokens: bfloat16 [8192, 2048], P('seq'), may hold values from -6 to 6
- input_heads: bfloat16 [8192, 4096], P('seq', 'tp'), may hold values from -6 to 6
- z_gate: bfloat16 [8192, 4096], P('seq', 'tp'), may hold values from -6 to 6
- b_proj: bfloat16 [8192, 128], P('seq'), may hold values from -0.5 to 0.5
- c_proj: bfloat16 [8192, 128], P('seq'), may hold values from -0.5 to 0.5
- step_size: float32 [8192, 64], P('seq', 'tp'), may hold values from 0.5 to 2
- decay_log: float32 [8192, 64], P('seq', 'tp'), as said below
- skip_gain: float32 [64], P('tp'), may hold values from 0.5 to 2
- init_state: float32 [64, 64, 128], P('tp'), may hold values from -48 to 48
- norm_gain: float32 [4096], P('tp'), may hold values from 0.1 to 1.9
- out_weight: bfloat16 [4096, 2048], P('tp'), may hold values from -0.09375 to 0.09375
- moe_gain: float32 [2048], replicated, may hold values from 0.1 to 1.9
- routes: int32 [8192, 2], P('seq'), may hold values from 0 to 63, all different within a row; in each aligned block of 128 rows (0 to 127, 128 to 255, ...) at most 8 rows name the same one
- route_weights: float32 [8192, 2], P('seq'), may hold values from 0.2 to 1
- w_gate: bfloat16 [64, 2048, 2048], P('seq', None, 'tp'), may hold values from -0.125 to 0.125
- w_up: bfloat16 [64, 2048, 2048], P('seq', None, 'tp'), may hold values from -0.125 to 0.125
- w_down: bfloat16 [64, 2048, 2048], P('seq', 'tp'), may hold values from -0.125 to 0.125
Outputs:
- mixed_out: bfloat16 [8192, 2048], P('seq', 'tp')
Inputs may be any that keep to these rules, and one draw needn't show every extreme that they name: `decay_log`: every entry is negative. `routes`: the two experts of a row differ. In each aligned block of 128 rows (the rows of one device) no expert is named by more than 8 rows, a bound that some block reaches.
All inputs are finite; a program needn't handle non-finite values.
Results may differ from a plain program's by a relative error of at most 0.02.
Values may be sent and summed in bfloat16 or wider, within the bound.
A program may use at most 128 MiB of HBM per device.

v0:
```python
import jax
import jax.numpy as jnp
from jax import lax
from jax.sharding import PartitionSpec as P


def entering(part, axis, combine, identity):
    place = lax.axis_index(axis)
    gathered = jax.tree.map(lambda a: lax.all_gather(a, axis), part)
    state = jax.tree.map(lambda a, e: jnp.zeros_like(a) + jnp.asarray(e, a.dtype), part, identity)

    def one(turn, state):
        return combine(
            state, jax.tree.map(lambda a: lax.dynamic_index_in_dim(a, turn, 0, False), gathered)
        )

    return lax.fori_loop(0, place, one, state)


def rms_rows(values, scale_gain):
    wide_vals = values.astype(jnp.float32)
    mean_sq = jnp.mean(wide_vals * wide_vals, axis=-1, keepdims=True)
    return (wide_vals * lax.rsqrt(mean_sq + 1e-05) * scale_gain).astype(jnp.bfloat16)


def merge_carry(first_part, second_part):
    decay_first, state_first = first_part
    decay_second, state_second = second_part
    return (decay_first * decay_second, decay_second[:, None, None] * state_first + state_second)


def body(
    tokens,
    input_heads,
    z_gate,
    b_proj,
    c_proj,
    step_size,
    decay_log,
    skip_gain,
    init_state,
    norm_gain,
    out_weight,
    moe_gain,
    routes,
    route_weights,
    w_gate,
    w_up,
    w_down,
):
    highest = lax.Precision.HIGHEST
    tok_rows = input_heads.shape[0]
    head_count = step_size.shape[1]
    head_size = init_state.shape[1]
    x_wide = input_heads.astype(jnp.float32).reshape(tok_rows, head_count, head_size)
    input_matrix_broad = b_proj.astype(jnp.float32)
    c_wide = c_proj.astype(jnp.float32)
    cum_decay = jnp.cumsum(decay_log, axis=0)
    end_decay = cum_decay[-1]
    positions = jnp.arange(tok_rows, dtype=jnp.int32)
    causal = positions[:, None] >= positions[None, :]
    scores = jnp.einsum("in,jn->ij", c_proj, b_proj, preferred_element_type=jnp.float32)
    cum_heads = cum_decay.T
    log_gap = cum_heads[:, :, None] - cum_heads[:, None, :]
    decay_mat = jnp.where(causal, jnp.exp(jnp.where(causal, log_gap, 0.0)), 0.0)
    mix_weights = decay_mat * scores[None] * step_size.T[:, None, :]
    intra_part = jnp.einsum("hij,jhp->ihp", mix_weights, x_wide, precision=highest)
    weighted = (jnp.exp(end_decay[None, :] - cum_decay) * step_size)[:, :, None] * x_wide
    local_state = jnp.einsum("jhp,jn->hpn", weighted, input_matrix_broad, precision=highest)
    block_decay = jnp.exp(end_decay)
    prior_decay, prior_state = entering(
        (block_decay, local_state),
        "seq",
        merge_carry,
        (jnp.ones_like(block_decay), jnp.zeros_like(local_state)),
    )
    arriving_rows = prior_decay[:, None, None] * init_state + prior_state
    inter_part = (
        jnp.einsum("in,hpn->ihp", c_wide, arriving_rows, precision=highest)
        * jnp.exp(cum_decay)[:, :, None]
    )
    ssd_out = intra_part + inter_part + skip_gain[None, :, None] * x_wide
    z_wide = z_gate.astype(jnp.float32).reshape(tok_rows, head_count, head_size)
    gated_vals = ssd_out * jax.nn.silu(z_wide)
    gated_vals = gated_vals * lax.rsqrt(
        jnp.mean(gated_vals * gated_vals, axis=2, keepdims=True) + 1e-05
    )
    normed = (gated_vals.reshape(tok_rows, head_count * head_size) * norm_gain).astype(jnp.bfloat16)
    partial_value = jnp.dot(normed, out_weight, preferred_element_type=jnp.float32)
    model_width = out_weight.shape[1]
    width_share = model_width // lax.axis_size("tp")
    col_start = lax.axis_index("tp") * width_share
    seq_count = lax.axis_size("seq")
    expert_count = w_gate.shape[0] * seq_count
    slot_count = 4 * tok_rows // seq_count
    top_count = routes.shape[1]
    flat_expert = routes.reshape(-1)
    onehot = (flat_expert[:, None] == jnp.arange(expert_count, dtype=jnp.int32)[None, :]).astype(
        jnp.int32
    )
    earlier_count = jnp.cumsum(onehot, axis=0) - onehot
    slot_rank = jnp.sum(earlier_count * onehot, axis=1)
    placed = flat_expert * slot_count + slot_rank
    owners = jnp.arange(top_count * tok_rows, dtype=jnp.int32) // top_count
    source = jnp.full((expert_count * slot_count,), tok_rows, jnp.int32).at[placed].set(owners)
    proj_sum = lax.psum(partial_value.astype(jnp.bfloat16), "tp").astype(jnp.float32)
    hidden_full = (tokens.astype(jnp.float32) + proj_sum).astype(jnp.bfloat16)
    moe_in = rms_rows(hidden_full, moe_gain)
    outgoing = jnp.take(moe_in, source, axis=0, mode="fill", fill_value=0).reshape(
        expert_count, slot_count, model_width
    )
    hidden = lax.dynamic_slice_in_dim(hidden_full, col_start, width_share, 1)
    moe_rows = lax.all_to_all(outgoing, "seq", split_axis=0, concat_axis=0, tiled=True)
    src_count, item_count, full_width = moe_rows.shape
    flat_rows = moe_rows.reshape(src_count * item_count, full_width)
    gate_val = jnp.dot(flat_rows, w_gate[0], preferred_element_type=jnp.float32)
    up_val = jnp.dot(flat_rows, w_up[0], preferred_element_type=jnp.float32)
    act_vals = (jax.nn.silu(gate_val) * up_val).astype(jnp.bfloat16)
    down_val = jnp.dot(act_vals, w_down[0], preferred_element_type=jnp.float32)
    summed = lax.psum_scatter(down_val.astype(jnp.bfloat16), "tp", scatter_dimension=1, tiled=True)
    results = summed.reshape(src_count, item_count, -1)
    returned = lax.all_to_all(results, "seq", split_axis=0, concat_axis=0, tiled=True)
    chosen_indices = jnp.take(
        returned.reshape(expert_count * slot_count, width_share), placed, axis=0
    ).reshape(tok_rows, top_count, width_share)
    mixed_out = hidden.astype(jnp.float32) + jnp.sum(
        route_weights[:, :, None] * chosen_indices.astype(jnp.float32), axis=1
    )
    return mixed_out.astype(jnp.bfloat16)


def solution(mesh):
    in_specs = (
        P("seq", None),
        P("seq", "tp"),
        P("seq", "tp"),
        P("seq", None),
        P("seq", None),
        P("seq", "tp"),
        P("seq", "tp"),
        P("tp"),
        P("tp", None, None),
        P("tp"),
        P("tp", None),
        P(),
        P("seq", None),
        P("seq", None),
        P("seq", None, "tp"),
        P("seq", None, "tp"),
        P("seq", "tp", None),
    )
    out_specs = P("seq", "tp")
    return jax.shard_map(body, mesh=mesh, in_specs=in_specs, out_specs=out_specs, check_vma=False)
```

profile of v0, /device:TPU:1, one launch (start us, length us, event | category | flops | bytes accessed | tf_op | source)
XLA Modules:
  0.0 428.5 jit_solution(1268096922327915747)
XLA Ops:
  6.5 0.0 all-gather.4.cloned.1.call-start
  6.6 0.9 copy.54
  7.5 0.2 reduce_window_sum.26
  7.7 0.8 copy.58
  8.6 0.1 copy.59
  8.6 1.1 copy.57
  9.8 2.0 fusion.34
  11.7 0.0 all-gather.4.cloned.1.call-update
  11.7 0.0 all-reduce.2.cloned.1.call-start
  11.8 0.1 copy.63
  11.9 0.1 eq.26
  12.0 0.1 reshape.134
  12.2 0.1 copy.60
  12.2 0.7 copy.55
  12.9 0.1 copy.61
  13.1 0.6 reduce-window.6
  13.7 0.2 slice_reduce_fusion
  13.9 0.1 copy.68
  14.1 0.1 mul.172
  14.2 0.1 fusion.49
  14.3 0.0 copy-start.13
  14.3 1.4 scatter_custom_fusion
  15.7 44.0 %all-gather.1 = f32[64,1,16]{2,1,0:T(1,128)S(1)} all-gather(f32[1,1,16]{2,1,0:T(1,128)S(1)} %get-tuple-element.60), channel_id=1, replica_groups=mesh['seq'=64,'tp'=4] {'seq'}, dimensions={0}, use_global_device_ids=true | all-gather | bytes 4160 | tf_op jit(solution)/shard_map/all_gather | solution.py:9
  59.8 0.6 iota_compare_fusion.2
  60.4 0.0 copy-done.5
  60.4 0.1 fusion.59
  60.5 97.7 %all-gather.4.cloned.1.call-done = f32[1024,64,128]{2,1,0:T(8,128)} async-done(((f32[16,64,128]{2,1,0:T(8,128)}), f32[1024,64,128]{2,1,0:T(8,128)}) %all-gather.4.cloned.1.call-update) | async-done | bytes 33554448 | tf_op jit(solution)/shard_map/all_gather | solution.py:9
  158.3 1.2 while.12
  158.3 1.2 bitcast_add_fusion.2
  159.5 1.5 fusion.20
  161.0 0.0 copy-start.12
  161.1 0.0 copy-start.1
  161.1 2.3 multiply_reduce_fusion.1
  163.5 0.2 fusion.35
  163.7 0.0 copy-start.3
  163.7 1.5 convolution_convert_fusion.1
  165.2 0.0 all-reduce.2.cloned.1.call-update
  165.3 0.0 reduce-scatter.2.cloned.1.call-start
  165.3 0.1 broadcast_in_dim.65
  165.4 117.4 %all-reduce.2.cloned.1.call-done = bf16[128,2048]{1,0:T(8,128)(2,1)} async-done(((bf16[128,2048]{1,0:T(8,128)(2,1)}), bf16[128,2048]{1,0:T(8,128)(2,1)}) %all-reduce.2.cloned.1.call-update) | async-done | bytes 524304 | tf_op jit(solution)/shard_map/psum | solution.py:106
  282.8 0.0 copy-done.3
  282.8 1.3 fusion.21
  284.1 0.2 fusion.23
  284.3 3.3 gather_fusion
  287.7 1.8 bitcast_select_fusion
  289.5 0.0 copy-start.16
  289.5 62.1 %all_to_all.10 = bf16[64,8,2048]{2,1,0:T(8,128)(2,1)S(1)} all-to-all(bf16[64,8,2048]{2,1,0:T(8,128)(2,1)S(1)} %bitcast_select_fusion), channel_id=1, replica_groups=mesh['seq'=64,'tp'=4] {'seq'}, dimensions={0} | all-to-all | bytes 4194304 | tf_op jit(solution)/shard_map/all_to_all | solution.py:113
  351.6 1.3 copy-done.2
  352.9 0.0 copy-done.16
  352.9 2.2 fusion.3
  355.1 0.0 copy-done
  355.1 6.3 %convolution_convert_fusion = bf16[512,2048]{1,0:T(8,128)(2,1)} fusion(bf16[1,512,2048]{2,1,0:T(8,128)(2,1)S(1)} %copy-done, bf16[1,2048,512]{2,1,0:T(8,128)(2,1)} %param.34, bf16[64,8,2048]{2,1,0:T(8,128)(2,1)} %copy-done.2, f32[512,512]{1,0:T(8,128)} %fusion.3), kind=kOutput, calls=%fused_computation.5 | convolution fusion | flops 2150105088 | bytes 9437184 | tf_op jit(solution)/shard_map/dot_general | solution.py:119
  361.4 0.0 reduce-scatter.2.cloned.1.call-update
  361.4 29.5 %reduce-scatter.2.cloned.1.call-done = bf16[512,512]{1,0:T(8,128)(2,1)} async-done(((bf16[512,2048]{1,0:T(8,128)(2,1)}), bf16[512,512]{1,0:T(8,128)(2,1)}) %reduce-scatter.2.cloned.1.call-update) | async-done | bytes 524304 | tf_op jit(solution)/shard_map/reduce_scatter | solution.py:120
  390.9 10.6 %all-to-all-start.1 = ((bf16[64,8,512]{2,1,0:T(8,128)(2,1)}), bf16[64,8,512]{2,1,0:T(8,128)(2,1)S(1)}, u32[]{:S(2)}, u32[]{:S(2)}) async-start(bf16[64,8,512]{2,1,0:T(8,128)(2,1)} %bitcast.100), calls=%async_computation.2 | async-start | bytes 1048576 | tf_op jit(solution)/shard_map/all_to_all | solution.py:122
  401.5 0.1 reduce_sum.42
  401.6 0.1 copy.66
  401.7 0.1 copy.67
  401.9 0.1 copy.62
  402.0 17.2 %all-to-all-done.1 = bf16[64,8,512]{2,1,0:T(8,128)(2,1)S(1)} async-done(((bf16[64,8,512]{2,1,0:T(8,128)(2,1)}), bf16[64,8,512]{2,1,0:T(8,128)(2,1)S(1)}, u32[]{:S(2)}, u32[]{:S(2)}) %all-to-all-start.1) | async-done | bytes 524320 | tf_op jit(solution)/shard_map/all_to_all | solution.py:122
  419.2 1.2 gather_fusion.1
  420.3 0.1 gather.15
  420.4 0.8 multiply_reduce_fusion
  421.3 0.7 add_convert_fusion.1
  (43 shorter events, 0.3 us)
Async XLA Ops:
  6.5 348.6 %copy-start = (bf16[1,512,2048]{2,1,0:T(8,128)(2,1)S(1)}, bf16[1,512,2048]{2,1,0:T(8,128)(2,1)}, u32[]{:S(2)}) copy-start(bf16[1,512,2048]{2,1,0:T(8,128)(2,1)} %param.35) | copy-start | bytes 6291460
  6.5 53.8 %copy-start.5 = (bf16[128,128]{1,0:T(8,128)(2,1)S(1)}, bf16[128,128]{1,0:T(8,128)(2,1)}, u32[]{:S(2)}) copy-start(bf16[128,128]{1,0:T(8,128)(2,1)} %param.22) | copy-start | bytes 98308
  6.5 5.2 %copy-start.9 = (s32[128,2]{0,1:T(2,128)S(1)}, s32[128,2]{0,1:T(2,128)}, u32[]{:S(2)}) copy-start(s32[128,2]{0,1:T(2,128)} %param.31) | copy-start | bytes 3076
  6.5 6.4 %copy-start.4 = (bf16[128,1024]{1,0:T(8,128)(2,1)S(1)}, bf16[128,1024]{1,0:T(8,128)(2,1)}, u32[]{:S(2)}) copy-start(bf16[128,1024]{1,0:T(8,128)(2,1)} %param.21) | copy-start | bytes 786436
  6.5 53.8 %copy-start.6 = (bf16[128,128]{1,0:T(8,128)(2,1)S(1)}, bf16[128,128]{1,0:T(8,128)(2,1)}, u32[]{:S(2)}) copy-start(bf16[128,128]{1,0:T(8,128)(2,1)} %param.23) | copy-start | bytes 98308
  6.5 151.7 %all-gather.4.cloned.1.call-start = ((), (), s32[]{:S(2)}) async-start(), calls=%async_computation.5 | async-start | bytes 34078720 | tf_op jit(solution)/shard_map/all_gather | solution.py:9
  11.7 271.1 %all-reduce.2.cloned.1.call-start = ((), (), s32[]{:S(2)}) async-start(), calls=%async_computation.3 | async-start | bytes 1048576 | tf_op jit(solution)/shard_map/psum | solution.py:106
  14.3 45.4 %copy-start.7 = (s32[256]{0:T(256)}, s32[256]{0:T(256)S(1)}, u32[]{:S(2)}) copy-start(s32[256]{0:T(256)S(1)} %fusion.49) | copy-start | bytes 3076
  14.3 143.9 %copy-start.13 = (s32[256,1]{0,1:T(1,128)}, s32[256,1]{0,1:T(1,128)S(1)}, u32[]{:S(2)}) copy-start(s32[256,1]{0,1:T(1,128)S(1)} %compare_select_fusion) | copy-start | bytes 3076
  161.0 2.4 copy-start.12
  161.1 2.6 copy-start.1
  163.7 119.1 %copy-start.3 = (bf16[128,2048]{1,0:T(8,128)(2,1)S(1)}, bf16[128,2048]{1,0:T(8,128)(2,1)}, u32[]{:S(2)}) copy-start(bf16[128,2048]{1,0:T(8,128)(2,1)} %param.19) | copy-start | bytes 1572868
  165.2 118.9 %copy-start.11 = (f32[2048]{0:T(1024)S(1)}, f32[2048]{0:T(1024)}, u32[]{:S(2)}) copy-start(f32[2048]{0:T(1024)} %param.30) | copy-start | bytes 24580
  165.3 225.6 %reduce-scatter.2.cloned.1.call-start = ((), (), s32[]{:S(2)}) async-start(), calls=%async_computation.4 | async-start | bytes 2621440 | tf_op jit(solution)/shard_map/reduce_scatter | solution.py:120
  289.5 63.4 %copy-start.16 = (bf16[1,2048,512]{2,1,0:T(8,128)(2,1)S(1)}, bf16[1,2048,512]{2,1,0:T(8,128)(2,1)}, u32[]{:S(2)}) copy-start(bf16[1,2048,512]{2,1,0:T(8,128)(2,1)} %param.33) | copy-start | bytes 6291460
  351.6 1.3 copy-start.2
  361.4 40.1 %copy-start.8 = (s32[256]{0:T(256)S(1)}, s32[256]{0:T(256)}, u32[]{:S(2)}) copy-start(s32[256]{0:T(256)} %copy-done.7) | copy-start | bytes 3076
  361.4 40.3 %copy-start.10 = (s32[128,2]{0,1:T(2,128)S(1)}, s32[128,2]{0,1:T(2,128)}, u32[]{:S(2)}) copy-start(s32[128,2]{0,1:T(2,128)} %param.31) | copy-start | bytes 3076
  361.4 40.5 %copy-start.15 = (f32[128,2]{0,1:T(2,128)S(1)}, f32[128,2]{0,1:T(2,128)}, u32[]{:S(2)}) copy-start(f32[128,2]{0,1:T(2,128)} %param.32) | copy-start | bytes 3076
  361.4 40.6 %copy-start.14 = (s32[256,1]{0,1:T(1,128)S(1)}, s32[256,1]{0,1:T(1,128)}, u32[]{:S(2)}) copy-start(s32[256,1]{0,1:T(1,128)} %copy-done.13) | copy-start | bytes 3076
  390.9 28.3 %all-to-all-start.1 = ((bf16[64,8,512]{2,1,0:T(8,128)(2,1)}), bf16[64,8,512]{2,1,0:T(8,128)(2,1)S(1)}, u32[]{:S(2)}, u32[]{:S(2)}) async-start(bf16[64,8,512]{2,1,0:T(8,128)(2,1)} %bitcast.100), calls=%async_computation.2 | async-start | bytes 1048576 | tf_op jit(solution)/shard_map/all_to_all | solution.py:122
Sparse Core Ops, SparseCore 0:
  11.8 146.3 all-gather.3
  165.4 117.3 all-reduce.1
  361.5 29.3 reduce-scatter.1
where the time goes:
time: 432 us; the launch traced here: 429 us
  waiting for transfers between devices  262 us (61%)
  blocking collectives  106 us (25%)
  matrix products  15.9 us (4%)
  between operations  13.5 us (3%)
  local copies, waits for them, and re-layouts  12.6 us (3%)
  starting transfers between devices  10.7 us (2%)
  other arithmetic  7.94 us (2%)
    psum x1, waiting for transfers between devices, body(): lax.psum(partial_value.astype(jnp.bfloat16), 'tp').astype(jnp.float32)  117 us
    all_gather x1, waiting for transfers between devices, entering(): gathered = jax.tree.map(lambda a: lax.all_gather(a, axis), part)  97.7 us
    all_to_all x1, blocking collectives, body(): lax.all_to_all(outgoing, 'seq', split_axis=0, concat_axis=0, tiled=True)  62.1 us
    all_gather x1, blocking collectives, entering(): gathered = jax.tree.map(lambda a: lax.all_gather(a, axis), part)  44 us
    reduce_scatter x1, waiting for transfers between devices, body(): lax.psum_scatter(down_val.astype(jnp.bfloat16), 'tp', scatter_dimension=1...  29.5 us
    all_to_all x1, waiting for transfers between devices, body(): lax.all_to_all(results, 'seq', split_axis=0, concat_axis=0, tiled=True)  17.2 us
    all_to_all x1, starting transfers between devices, body(): lax.all_to_all(results, 'seq', split_axis=0, concat_axis=0, tiled=True)  10.6 us
  transfers between devices with their start and end apart: 4, of which 4 were waited for; matrix products, arithmetic and copies ran while one was open for 1% of the time, Pallas kernels for 0%

commit v1 on v0

--- a/solution.py
+++ b/solution.py
@@ -103,7 +103,9 @@
     placed = flat_expert * slot_count + slot_rank
     owners = jnp.arange(top_count * tok_rows, dtype=jnp.int32) // top_count
     source = jnp.full((expert_count * slot_count,), tok_rows, jnp.int32).at[placed].set(owners)
-    proj_sum = lax.psum(partial_value.astype(jnp.bfloat16), "tp").astype(jnp.float32)
+    proj_sum = jnp.sum(lax.all_gather(partial_value.astype(jnp.bfloat16), "tp"), axis=0).astype(
+        jnp.float32
+    )
     hidden_full = (tokens.astype(jnp.float32) + proj_sum).astype(jnp.bfloat16)
     moe_in = rms_rows(hidden_full, moe_gain)
     outgoing = jnp.take(moe_in, source, axis=0, mode="fill", fill_value=0).reshape(

time: 432 us -> 419 us (0.970)
  waiting for transfers between devices: 262 us -> 248 us
    psum x1 -> x0, waiting for transfers between devices: 117 us -> none  [body(): lax.psum(partial_value.astype(jnp.bfloat16), 'tp').astype(jnp.float32)]
    all_gather x0 -> x1, waiting for transfers between devices: none -> 101 us  [body(): lax.all_gather(partial_value.astype(jnp.bfloat16), 'tp')]
where the time goes in v1:
time: 419 us; the launch traced here: 415 us
  waiting for transfers between devices  248 us (59%)
  blocking collectives  104 us (25%)
  matrix products  15.9 us (4%)
  between operations  13.4 us (3%)
  local copies, waits for them, and re-layouts  12.6 us (3%)
  starting transfers between devices  10.7 us (3%)
  other arithmetic  9.97 us (2%)
    all_gather x1, waiting for transfers between devices, body(): lax.all_gather(partial_value.astype(jnp.bfloat16), 'tp')  101 us
    all_gather x1, waiting for transfers between devices, entering(): gathered = jax.tree.map(lambda a: lax.all_gather(a, axis), part)  101 us
    all_to_all x1, blocking collectives, body(): lax.all_to_all(outgoing, 'seq', split_axis=0, concat_axis=0, tiled=True)  60.3 us
    all_gather x1, blocking collectives, entering(): gathered = jax.tree.map(lambda a: lax.all_gather(a, axis), part)  44 us
    reduce_scatter x1, waiting for transfers between devices, body(): lax.psum_scatter(down_val.astype(jnp.bfloat16), 'tp', scatter_dimension=1...  28.9 us
    all_to_all x1, waiting for transfers between devices, body(): lax.all_to_all(results, 'seq', split_axis=0, concat_axis=0, tiled=True)  17.2 us
    all_to_all x1, starting transfers between devices, body(): lax.all_to_all(results, 'seq', split_axis=0, concat_axis=0, tiled=True)  10.6 us
  transfers between devices with their start and end apart: 4, of which 4 were waited for; matrix products, arithmetic and copies ran while one was open for 1% of the time, Pallas kernels for 0%

profile of v1, /device:TPU:1, one launch (start us, length us, event | category | flops | bytes accessed | tf_op | source)
XLA Modules:
  0.0 415.4 jit_solution(14350686415505870814)
XLA Ops:
  6.5 0.0 copy-start
  6.5 0.0 all-gather.6.cloned.1.call-start
  6.6 1.0 copy.54
  7.6 0.2 reduce_window_sum.26
  7.7 0.8 copy.58
  8.6 0.1 copy.59
  8.6 1.1 copy.57
  9.8 1.9 fusion.34
  11.7 0.0 all-gather.6.cloned.1.call-update
  11.7 0.0 all-gather.8.cloned.1.call-start
  11.8 0.1 copy.60
  11.9 0.7 copy.55
  12.5 0.1 copy.61
  12.7 44.0 %all-gather.2 = f32[64,1,16]{2,1,0:T(1,128)S(1)} all-gather(f32[1,1,16]{2,1,0:T(1,128)S(1)} %get-tuple-element.60), channel_id=1, replica_groups=mesh['seq'=64,'tp'=4] {'seq'}, dimensions={0}, use_global_device_ids=true | all-gather | bytes 4160 | tf_op jit(solution)/shard_map/all_gather | solution.py:9
  56.7 0.6 iota_compare_fusion.2
  57.3 0.0 copy-done.4
  57.3 0.1 fusion.59
  57.4 100.8 %all-gather.6.cloned.1.call-done = f32[1024,64,128]{2,1,0:T(8,128)} async-done(((f32[16,64,128]{2,1,0:T(8,128)}), f32[1024,64,128]{2,1,0:T(8,128)}) %all-gather.6.cloned.1.call-update) | async-done | bytes 33554448 | tf_op jit(solution)/shard_map/all_gather | solution.py:9
  158.3 0.0 copy-start.11
  158.3 1.2 while.12
  158.4 1.2 bitcast_add_fusion.2
  159.6 1.5 fusion.20
  161.1 0.0 copy-start.8
  161.1 0.0 copy-start.1
  161.1 2.3 multiply_reduce_fusion.1
  163.5 0.2 fusion.35
  163.8 0.0 copy-start.6
  163.8 1.5 convolution_convert_fusion.1
  165.3 0.0 all-gather.8.cloned.1.call-update
  165.3 0.0 reduce-scatter.2.cloned.1.call-start
  165.4 0.1 copy.63
  165.5 0.1 eq.26
  165.6 0.1 reshape.134
  165.8 0.6 reduce-window.6
  166.4 0.2 slice_reduce_fusion
  166.6 0.1 copy.68
  166.8 0.1 mul.172
  166.9 0.1 fusion.49
  167.0 1.4 scatter_custom_fusion
  168.5 0.1 broadcast_in_dim.65
  168.6 101.5 %all-gather.8.cloned.1.call-done = bf16[512,2048]{1,0:T(8,128)(2,1)} async-done(((bf16[128,2048]{1,0:T(8,128)(2,1)}), bf16[512,2048]{1,0:T(8,128)(2,1)}) %all-gather.8.cloned.1.call-update) | async-done | bytes 2097168 | tf_op jit(solution)/shard_map/all_gather | solution.py:106
  270.0 2.0 reduce_sum.53
  272.1 1.3 fusion.21
  273.4 0.2 fusion.23
  273.6 3.3 gather_fusion
  277.0 1.8 bitcast_select_fusion
  278.8 0.0 copy-start.10
  278.8 60.3 %all_to_all.10 = bf16[64,8,2048]{2,1,0:T(8,128)(2,1)S(1)} all-to-all(bf16[64,8,2048]{2,1,0:T(8,128)(2,1)S(1)} %bitcast_select_fusion), channel_id=1, replica_groups=mesh['seq'=64,'tp'=4] {'seq'}, dimensions={0} | all-to-all | bytes 4194304 | tf_op jit(solution)/shard_map/all_to_all | solution.py:115
  339.0 1.3 copy-done.2
  340.3 2.2 fusion.3
  342.6 0.0 copy-done
  342.6 6.3 %convolution_convert_fusion = bf16[512,2048]{1,0:T(8,128)(2,1)} fusion(bf16[1,512,2048]{2,1,0:T(8,128)(2,1)S(1)} %copy-done, bf16[1,2048,512]{2,1,0:T(8,128)(2,1)} %param.34, bf16[64,8,2048]{2,1,0:T(8,128)(2,1)} %copy-done.2, f32[512,512]{1,0:T(8,128)} %fusion.3), kind=kOutput, calls=%fused_computation.5 | convolution fusion | flops 2150105088 | bytes 9437184 | tf_op jit(solution)/shard_map/dot_general | solution.py:121
  348.8 0.0 reduce-scatter.2.cloned.1.call-update
  348.9 28.9 %reduce-scatter.2.cloned.1.call-done = bf16[512,512]{1,0:T(8,128)(2,1)} async-done(((bf16[512,2048]{1,0:T(8,128)(2,1)}), bf16[512,512]{1,0:T(8,128)(2,1)}) %reduce-scatter.2.cloned.1.call-update) | async-done | bytes 524304 | tf_op jit(solution)/shard_map/reduce_scatter | solution.py:122
  377.7 10.6 %all-to-all-start.1 = ((bf16[64,8,512]{2,1,0:T(8,128)(2,1)}), bf16[64,8,512]{2,1,0:T(8,128)(2,1)S(1)}, u32[]{:S(2)}, u32[]{:S(2)}) async-start(bf16[64,8,512]{2,1,0:T(8,128)(2,1)} %bitcast.102), calls=%async_computation.2 | async-start | bytes 1048576 | tf_op jit(solution)/shard_map/all_to_all | solution.py:124
  388.3 0.1 reduce_sum.55
  388.5 0.1 copy.66
  388.6 0.1 copy.67
  388.7 0.1 copy.62
  388.8 17.2 %all-to-all-done.1 = bf16[64,8,512]{2,1,0:T(8,128)(2,1)S(1)} async-done(((bf16[64,8,512]{2,1,0:T(8,128)(2,1)}), bf16[64,8,512]{2,1,0:T(8,128)(2,1)S(1)}, u32[]{:S(2)}, u32[]{:S(2)}) %all-to-all-start.1) | async-done | bytes 524320 | tf_op jit(solution)/shard_map/all_to_all | solution.py:124
  406.0 1.2 gather_fusion.1
  407.2 0.1 gather.15
  407.3 0.8 multiply_reduce_fusion
  408.2 0.7 add_convert_fusion.1
  (34 shorter events, 0.3 us)
Async XLA Ops:
  6.5 336.0 %copy-start = (bf16[1,512,2048]{2,1,0:T(8,128)(2,1)S(1)}, bf16[1,512,2048]{2,1,0:T(8,128)(2,1)}, u32[]{:S(2)}) copy-start(bf16[1,512,2048]{2,1,0:T(8,128)(2,1)} %param.35) | copy-start | bytes 6291460
  6.5 50.8 %copy-start.4 = (bf16[128,128]{1,0:T(8,128)(2,1)S(1)}, bf16[128,128]{1,0:T(8,128)(2,1)}, u32[]{:S(2)}) copy-start(bf16[128,128]{1,0:T(8,128)(2,1)} %param.22) | copy-start | bytes 98308
  6.5 6.0 %copy-start.3 = (bf16[128,1024]{1,0:T(8,128)(2,1)S(1)}, bf16[128,1024]{1,0:T(8,128)(2,1)}, u32[]{:S(2)}) copy-start(bf16[128,1024]{1,0:T(8,128)(2,1)} %param.21) | copy-start | bytes 786436
  6.5 50.8 %copy-start.5 = (bf16[128,128]{1,0:T(8,128)(2,1)S(1)}, bf16[128,128]{1,0:T(8,128)(2,1)}, u32[]{:S(2)}) copy-start(bf16[128,128]{1,0:T(8,128)(2,1)} %param.23) | copy-start | bytes 98308
  6.5 151.7 %all-gather.6.cloned.1.call-start = ((), (), s32[]{:S(2)}) async-start(), calls=%async_computation.4 | async-start | bytes 34078720 | tf_op jit(solution)/shard_map/all_gather | solution.py:9
  11.7 258.3 %all-gather.8.cloned.1.call-start = ((), (), s32[]{:S(2)}) async-start(), calls=%async_computation.5 | async-start | bytes 2621440 | tf_op jit(solution)/shard_map/all_gather | solution.py:106
  158.3 2.8 copy-start.11
  161.1 2.4 copy-start.8
  161.1 2.6 copy-start.1
  163.8 1.6 copy-start.6
  165.3 212.4 %reduce-scatter.2.cloned.1.call-start = ((), (), s32[]{:S(2)}) async-start(), calls=%async_computation.3 | async-start | bytes 2621440 | tf_op jit(solution)/shard_map/reduce_scatter | solution.py:122
  270.0 3.4 copy-start.7
  278.8 61.6 %copy-start.10 = (bf16[1,2048,512]{2,1,0:T(8,128)(2,1)S(1)}, bf16[1,2048,512]{2,1,0:T(8,128)(2,1)}, u32[]{:S(2)}) copy-start(bf16[1,2048,512]{2,1,0:T(8,128)(2,1)} %param.33) | copy-start | bytes 6291460
  339.0 1.3 copy-start.2
  348.8 39.9 %copy-start.9 = (f32[128,2]{0,1:T(2,128)S(1)}, f32[128,2]{0,1:T(2,128)}, u32[]{:S(2)}) copy-start(f32[128,2]{0,1:T(2,128)} %param.32) | copy-start | bytes 3076
  377.7 28.3 %all-to-all-start.1 = ((bf16[64,8,512]{2,1,0:T(8,128)(2,1)}), bf16[64,8,512]{2,1,0:T(8,128)(2,1)S(1)}, u32[]{:S(2)}, u32[]{:S(2)}) async-start(bf16[64,8,512]{2,1,0:T(8,128)(2,1)} %bitcast.102), calls=%async_computation.2 | async-start | bytes 1048576 | tf_op jit(solution)/shard_map/all_to_all | solution.py:124
Sparse Core Ops, SparseCore 0:
  11.9 146.3 all-gather.5
  165.5 104.5 all-gather.7
  349.0 28.6 reduce-scatter.1
